TPU v7x, 512 devices: a whole 4x4x16 slice. The times are simulated.
512 devices in a mesh: wide: 32 (over x, z_hi, core), narrow: 16 (over z_lo, y).
Axes of the slice: x: 4, y: 4, z: 16 (z_hi: 4, z_lo: 4; z = z_hi * 4 + z_lo), core: 2. Of those that a mesh axis runs over, the one named last changes fastest.
Arguments:
- local_slopes: float32 [512, 512, 128], P(('wide', 'narrow')), may hold values from -0.25 to 0.25
- global_slopes: float32 [512, 512, 1024], P(('wide', 'narrow')), may hold values from -0.25 to 0.25
- residuals: float32 [512, 512], P(('wide', 'narrow')), may hold values from -6 to 6
- weights: float32 [512, 512], P(('wide', 'narrow')), may hold values from 0.1 to 10
- track_slot_count: int32 [512], P(('wide', 'narrow')), may hold values from 64 to 512
- windows: int32 [512], P(('wide', 'narrow')), may hold values from 0 to 3
Outputs:
- normal_matrix: float32 [4, 1024, 1024], P(None, 'narrow', 'wide')
- normal_rhs: float32 [4, 1024], P(None, 'narrow')
All inputs are finite; a program needn't handle non-finite values.
Results may differ from a plain program's by a relative error of at most 0.0003.
Values sent between devices are 32-bit elements; how exact they have to be, the bound alone decides.
No kernel may reach another device: no remote copies, remote signals or barrier semaphores. Data moves between devices by JAX's collectives and lax.ppermute only.
A program may use at most 64 MiB of HBM per device.

v0:
```python
import jax
import jax.numpy as jnp
from jax import lax
from jax.experimental import pallas as pl
from jax.experimental.pallas import tpu as pltpu
from jax.sharding import Mesh
from jax.sharding import PartitionSpec as P

NWIN = 4
AXES = ("wide_0", "wide_1", "wide_2", "narrow_0", "narrow_1")
ALL = ("wide_0", "wide_1", "wide_2", "narrow_0", "narrow_1")
PLANE = ("wide_0", "narrow_1", "wide_2")
RING = ("wide_1", "narrow_0")
HI = lax.Precision.HIGHEST
F32 = jnp.float32


def tdot(left, right):
    return lax.dot_general(
        left, right, (((0,), (0,)), ((), ())), precision=HI, preferred_element_type=F32
    )


def iota(shape, dim):
    return lax.broadcasted_iota(jnp.int32, shape, dim)


def inverse(curv):
    size = 32
    lane, sub = iota((size, 128), 1), iota((size, 128), 0)
    rows = [curv[k * size : (k + 1) * size, :] for k in range(4)]
    for k in range(4):
        panel = rows[k]
        for t in range(size):
            at = k * size + t
            column = panel[:, at : at + 1]
            pivot = 1.0 / panel[t : t + 1, at : at + 1]
            fresh = jnp.where(lane[:1] == at, pivot, panel[t : t + 1, :] * pivot)
            panel = jnp.where(sub == t, fresh, jnp.where(lane == at, 0.0, panel) - column * fresh)
        others = [o for o in range(4) if o != k]
        rest = jnp.concatenate([rows[o] for o in others], axis=0)
        factor = rest[:, k * size : (k + 1) * size]
        inside = (iota((96, 128), 1) // size) == k
        rest = jnp.where(inside, 0.0, rest) - jnp.dot(
            factor, panel, precision=HI, preferred_element_type=F32
        )
        for n, o in enumerate(others):
            rows[o] = rest[n * size : (n + 1) * size, :]
        rows[k] = panel
    return jnp.concatenate(rows, axis=0)


def pick_lanes(pieces):
    place = iota(pieces[0].shape, 1) // 32
    out = pieces[3]
    for b in (2, 1, 0):
        out = jnp.where(place == b, pieces[b], out)
    return out


def roll32(value, by):
    by %= 4
    return value if by == 0 else pltpu.roll(value, by * 32, 1)


def assemble_kernel(count, window, weight, resid, local, glob, out, gp, vgp, matrix):
    live = jnp.where(iota((1, 512), 1) < count[0], weight[...], 0.0)
    vb = jnp.transpose(jnp.broadcast_to(live, (128, 512)))
    rb = jnp.transpose(jnp.broadcast_to(resid[...], (128, 512)))
    slopes = local[...]
    wl = slopes * vb
    curv = tdot(wl, slopes)
    curv = curv + jnp.where(iota((128, 128), 0) == iota((128, 128), 1), 1.0, 0.0)

    for x in range(4):
        for h in range(8):
            r = slice(h * 64, h * 64 + 64)
            first = glob[r, x * 256 : x * 256 + 128]
            second = glob[r, x * 256 + 128 : x * 256 + 256]
            even = pick_lanes([first, roll32(first, -1), roll32(second, 2), roll32(second, 1)])
            odd = pick_lanes([roll32(first, -1), roll32(first, 2), roll32(second, 1), second])
            gp[r, x * 128 : x * 128 + 128] = even
            gp[r, 512 + x * 128 : 512 + x * 128 + 128] = odd
            vgp[r, x * 128 : x * 128 + 128] = even * vb[r]
            vgp[r, 512 + x * 128 : 512 + x * 128 + 128] = odd * vb[r]

    coupling = tdot(wl, gp[...])
    lr = tdot(wl, rb)
    inv = inverse(curv)
    solved = jnp.dot(inv, coupling, precision=HI, preferred_element_type=F32)

    rhs = []
    for c in range(8):
        cols = slice(c * 128, c * 128 + 128)
        rhs.append(
            jnp.sum(vgp[:, cols] * rb, axis=0, keepdims=True)
            - jnp.sum(solved[:, cols] * lr, axis=0, keepdims=True)
        )

    for q in range(2):
        for jh in range(2):
            n = slice((q * 2 + jh) * 256, (q * 2 + jh) * 256 + 256)
            for p in range(2):
                for ih in range(2):
                    if (p == q and ih > jh) or (p != q and ih < jh):
                        continue
                    m = slice((p * 2 + ih) * 256, (p * 2 + ih) * 256 + 256)
                    matrix[m, n] = tdot(vgp[:, m], gp[:, n]) - tdot(solved[:, m], coupling[:, n])

    place = iota((32, 128), 1) // 32
    below = iota((32, 128), 0) >= iota((32, 128), 1) % 32
    ondiag = iota((32, 128), 0) == iota((32, 128), 1) % 32
    sub8 = iota((8, 128), 0)
    own = jnp.broadcast_to(window[0].astype(F32), (8, 128))
    for x in range(4):
        for y in range(4):
            extra = [pick_lanes([roll32(rhs[p * 4 + z], z - y) for z in range(4)]) for p in range(2)]
            i = x * 4 + y
            pair = matrix[512 + i * 32 : 512 + i * 32 + 32, x * 128 : x * 128 + 128]
            held = jnp.where(ondiag & (place == y), pair, 0.0)
            edge = roll32(jnp.sum(held, axis=0, keepdims=True), -y)
            tail = jnp.where(
                sub8 == 0,
                extra[0],
                jnp.where(sub8 == 1, extra[1], jnp.where(sub8 == 2, edge, own)),
            )
            for q in range(2):
                dest = (x * 4 + y) * 2 + q
                cols = slice(q * 512 + x * 128, q * 512 + x * 128 + 128)
                for z in range(4):
                    i = z * 4 + y
                    same = slice(q * 512 + i * 32, q * 512 + i * 32 + 32)
                    cross = slice((1 - q) * 512 + i * 32, (1 - q) * 512 + i * 32 + 32)
                    if i < x * 4:
                        tile = matrix[same, cols]
                    elif i > x * 4 + 3:
                        tile = matrix[cross, cols]
                    else:
                        j = place + x * 4
                        tile = jnp.where(
                            (j > i) | ((j == i) & below), matrix[same, cols], matrix[cross, cols]
                        )
                    out[dest, z * 32 : z * 32 + 32, :] = tile
                out[dest, 128:136, :] = tail


def windows_kernel(arrived, out):
    def sums(g):
        acc = [jnp.zeros((8, 128), F32) for _ in range(NWIN)]
        for s in range(32):
            block = arrived[s, pl.ds(g * 8, 8), :]
            which = jnp.broadcast_to(arrived[s, 131:132, :], (8, 128))
            for w in range(NWIN):
                acc[w] = acc[w] + jnp.where(which == float(w), block, 0.0)
        return acc

    @pl.loop(0, 4)
    def _(z):
        for k in range(4):
            acc = sums(z * 4 + k)
            for b in range(4):
                out[b * 4 + z, k * 8 : k * 8 + 8, :] = pick_lanes(
                    [roll32(acc[w], w - b) for w in range(NWIN)]
                )

    acc = sums(16)
    packed = [pick_lanes([roll32(acc[w], w - b) for w in range(NWIN)]) for b in range(4)]
    for z in range(4):
        tail = jnp.where(iota((8, 128), 0) == 2, packed[0], packed[z])
        for b in range(4):
            out[b * 4 + z, 32:40, :] = tail


def ring_kernel(arrived, out):
    total = arrived[0]
    for s in range(1, 16):
        total = total + arrived[s]
    out[...] = total


def finish_kernel(mine, other, out, rhs):
    x, zh, q = lax.axis_index("wide_0"), lax.axis_index("wide_1"), lax.axis_index("wide_2")
    zl, y = lax.axis_index("narrow_0"), lax.axis_index("narrow_1")
    i, j = zl * 4 + y, x * 4 + zh
    diag = jnp.broadcast_to(i == j, (32, 32))
    half = jnp.where(i <= j, q, 1 - q)
    lower = jnp.broadcast_to(half == 0, (32, 32))
    a, b = iota((32, 32), 0), iota((32, 32), 1)
    turned = jnp.transpose(mine[0:32, :])
    for w in range(NWIN):
        cols = slice(w * 32, w * 32 + 32)
        held, theirs = mine[0:32, cols], other[0:32, cols]
        flip = turned[cols, :]
        edge = jnp.broadcast_to(mine[34:35, cols], (32, 32))
        own_part = jnp.where(diag & (a >= b), held, flip)
        other_part = jnp.where(diag & (a == b), edge, jnp.where(diag & (a > b), flip, theirs))
        out[w, :, 0:32] = jnp.where(lower, own_part, other_part)
        out[w, :, 32:64] = jnp.where(lower, other_part, own_part)
        rhs[w : w + 1, 0:32] = mine[32:33, cols]
        rhs[w : w + 1, 32:64] = mine[33:34, cols]


def vmem(count):
    return [pl.BlockSpec(memory_space=pltpu.VMEM)] * count


def turn_pairs():
    place = lambda x, zh, q, zl, y: (((x * 4 + zh) * 2 + q) * 4 + zl) * 4 + y
    pairs = []
    for x in range(4):
        for zh in range(4):
            for q in range(2):
                for zl in range(4):
                    for y in range(4):
                        i, j = zl * 4 + y, x * 4 + zh
                        p = q if i <= j else 1 - q
                        target = 1 - q if i == j else p
                        pairs.append((place(x, zh, q, zl, y), place(zl, y, target, x, zh)))
    return pairs


def on_device(local_slopes, global_slopes, residuals, weights, track_slot_count, windows):
    big = pltpu.CompilerParams(vmem_limit_bytes=48 << 20)
    payload = pl.pallas_call(
        assemble_kernel,
        out_shape=jax.ShapeDtypeStruct((32, 136, 128), F32),
        in_specs=[pl.BlockSpec(memory_space=pltpu.SMEM)] * 2 + vmem(4),
        out_specs=vmem(1)[0],
        scratch_shapes=[
            pltpu.VMEM((512, 1024), F32),
            pltpu.VMEM((512, 1024), F32),
            pltpu.VMEM((1024, 1024), F32),
        ],
        compiler_params=big,
        name="assemble",
    )(track_slot_count, windows, weights, residuals, local_slopes[0], global_slopes[0])
    arrived = lax.all_to_all(payload, PLANE, split_axis=0, concat_axis=0, tiled=True)
    packed = pl.pallas_call(
        windows_kernel,
        out_shape=jax.ShapeDtypeStruct((16, 40, 128), F32),
        in_specs=vmem(1),
        out_specs=vmem(1)[0],
        compiler_params=big,
        name="window_sums",
    )(arrived)
    ring = lax.all_to_all(packed, RING, split_axis=0, concat_axis=0, tiled=True)
    mine = pl.pallas_call(
        ring_kernel,
        out_shape=jax.ShapeDtypeStruct((40, 128), F32),
        in_specs=vmem(1),
        out_specs=vmem(1)[0],
        name="ring_sums",
    )(ring)
    other = lax.ppermute(mine, ALL, turn_pairs())
    out, rhs = pl.pallas_call(
        finish_kernel,
        out_shape=(
            jax.ShapeDtypeStruct((NWIN, 32, 64), F32),
            jax.ShapeDtypeStruct((NWIN, 64), F32),
        ),
        in_specs=vmem(2),
        out_specs=tuple(vmem(2)),
        name="finish",
    )(mine, other)
    return jnp.transpose(out, (0, 2, 1)), rhs


def solution(mesh):
    split = Mesh(mesh.devices.reshape(4, 4, 2, 4, 4), AXES)
    return jax.shard_map(
        on_device,
        mesh=split,
        in_specs=(
            P(AXES, None, None),
            P(AXES, None, None),
            P(AXES, None),
            P(AXES, None),
            P(AXES),
            P(AXES),
        ),
        out_specs=(
            P(None, ("narrow_0", "narrow_1"), ("wide_0", "wide_1", "wide_2")),
            P(None, ("narrow_0", "narrow_1")),
        ),
        check_vma=False,
    )
```

profile of v0, /device:TPU:16, one launch (start us, length us, event | category | flops | bytes accessed | tf_op | source)
XLA Modules:
  0.0 120.7 jit_solution(6018525100691194383)
XLA Ops:
  1.9 0.0 copy-start
  1.9 1.6 %copy-done = f32[1,512,1024]{2,1,0:T(8,128)S(1)} copy-done((f32[1,512,1024]{2,1,0:T(8,128)S(1)}, f32[1,512,1024]{2,1,0:T(8,128)}, u32[]{:S(2)}) %copy-start) | copy-done | bytes 2097176
  3.5 0.0 copy-start.1
  3.5 0.9 copy-done.1
  4.5 0.0 copy-start.2
  4.5 0.7 copy-done.2
  5.1 0.0 copy-start.3
  5.1 0.7 copy-done.3
  5.8 21.2 %assemble.1 = f32[32,136,128]{2,1,0:T(8,128)S(1)} custom-call(s32[1]{0:T(128)S(6)} %copy.8.count, s32[1]{0:T(128)S(6)} %copy.9.window, f32[1,512]{1,0:T(1,128)S(1)} %copy-done.2, f32[1,512]{1,0:T(1,128)S(1)} %copy-done.3, f32[512,128]{1,0:T(8,128)S(1)} %bitcast.4, f32[512,1024]{1,0:T(8,128)S(1)} %bitcast.3), custom_call_target="tpu_custom_call" | custom-call | tf_op jit(solution)/shard_map/assemble/pallas_call | solution.py:224
  27.0 36.4 %all_to_all.10.arrived = f32[32,136,128]{2,1,0:T(8,128)S(1)} all-to-all(f32[32,136,128]{2,1,0:T(8,128)S(1)} %assemble.1), channel_id=1, replica_groups=mesh['wide_0'=4,'wide_1'=4,'wide_2'=2,'narrow_0'=4,'narrow_1'=4] {'wide_..., dimensions={0} | all-to-all | bytes 4456448 | tf_op jit(solution)/shard_map/all_to_all | solution.py:237
  63.4 1.3 %window_sums.1 = f32[16,40,128]{2,1,0:T(8,128)S(1)} custom-call(f32[32,136,128]{2,1,0:T(8,128)S(1)} %all_to_all.10.arrived), custom_call_target="tpu_custom_call" | custom-call | tf_op jit(solution)/shard_map/window_sums/pallas_call | solution.py:238
  64.7 35.3 %all_to_all.11.arrived = f32[16,40,128]{2,1,0:T(8,128)} all-to-all(f32[16,40,128]{2,1,0:T(8,128)S(1)} %window_sums.1), channel_id=1, replica_groups=mesh['wide_0'=4,'wide_1'=4,'wide_2'=2,'narrow_0'=4,'narrow_1'=4] {'wide_..., dimensions={0} | all-to-all | bytes 655360 | tf_op jit(solution)/shard_map/all_to_all | solution.py:246
  99.9 1.6 %ring_sums.1.mine = f32[40,128]{1,0:T(8,128)} custom-call(f32[16,40,128]{2,1,0:T(8,128)} %all_to_all.11.arrived), custom_call_target="tpu_custom_call" | custom-call | tf_op jit(solution)/shard_map/ring_sums/pallas_call | solution.py:247
  101.5 7.9 %collective-permute-start = (f32[40,128]{1,0:T(8,128)}, f32[40,128]{1,0:T(8,128)S(1)}, u32[]{:S(2)}, u32[]{:S(2)}) collective-permute-start(f32[40,128]{1,0:T(8,128)} %ring_sums.1.mine), channel_id=1, source_target_pairs={{0,16},{1,48},{2,80},{3,112},{4,144},{5,176},{6,208},{7,240},{8,27... | collective-permute-start | bytes 61448 | tf_op jit(solution)/shard_map/ppermute | solution.py:254
  109.4 9.1 %collective-permute-done.other = f32[40,128]{1,0:T(8,128)S(1)} collective-permute-done((f32[40,128]{1,0:T(8,128)}, f32[40,128]{1,0:T(8,128)S(1)}, u32[]{:S(2)}, u32[]{:S(2)}) %collective-permute-start) | collective-permute-done | bytes 20512 | tf_op jit(solution)/shard_map/ppermute | solution.py:254
  118.5 0.0 copy-start.4
  118.5 0.6 copy-done.4
  119.1 1.6 %finish.1 = (f32[4,32,64]{2,1,0:T(8,128)}, f32[4,64]{1,0:T(4,128)}) custom-call(f32[40,128]{1,0:T(8,128)} %ring_sums.1.mine, f32[40,128]{1,0:T(8,128)} %copy-done.4), custom_call_target="tpu_custom_call" | custom-call | tf_op jit(solution)/shard_map/finish/pallas_call | solution.py:255
Async XLA Ops:
  1.9 1.6 %copy-start = (f32[1,512,1024]{2,1,0:T(8,128)S(1)}, f32[1,512,1024]{2,1,0:T(8,128)}, u32[]{:S(2)}) copy-start(f32[1,512,1024]{2,1,0:T(8,128)} %param.7) | copy-start | bytes 6291460
  3.5 0.9 copy-start.1
  4.5 0.7 copy-start.2
  5.1 0.7 copy-start.3
  101.5 17.0 %collective-permute-start = (f32[40,128]{1,0:T(8,128)}, f32[40,128]{1,0:T(8,128)S(1)}, u32[]{:S(2)}, u32[]{:S(2)}) collective-permute-start(f32[40,128]{1,0:T(8,128)} %ring_sums.1.mine), channel_id=1, source_target_pairs={{0,16},{1,48},{2,80},{3,112},{4,144},{5,176},{6,208},{7,240},{8,27... | collective-permute-start | bytes 61448 | tf_op jit(solution)/shard_map/ppermute | solution.py:254
  118.5 0.6 copy-start.4
where the time goes:
time: 121 us
  blocking collectives  71.7 us (59%)
  Pallas kernels  25.6 us (21%)
  waiting for transfers between devices  9.11 us (8%)
  starting transfers between devices  7.87 us (7%)
  local copies, waits for them, and re-layouts  4.5 us (4%)
  between operations  1.96 us (2%)
    all_to_all x1, blocking collectives, on_device(): lax.all_to_all(payload, PLANE, split_axis=0, concat_axis=0, tiled=True)  36.4 us
    all_to_all x1, blocking collectives, on_device(): ring = lax.all_to_all(packed, RING, split_axis=0, concat_axis=0, tiled=True)  35.3 us
    pallas_call x1, Pallas kernels, on_device(): pl.pallas_call(assemble_kernel, out_shape=jax.ShapeDtypeStruct((32, 136,...  21.2 us
    ppermute x1, waiting for transfers between devices, on_device(): other = lax.ppermute(mine, ALL, turn_pairs())  9.11 us
    ppermute x1, starting transfers between devices, on_device(): other = lax.ppermute(mine, ALL, turn_pairs())  7.87 us
    unnamed x10, local copies, waits for them, and re-layouts  4.5 us
  transfers between devices with their start and end apart: 1, of which 1 were waited for; matrix products, arithmetic and copies ran while one was open for 0% of the time, Pallas kernels for 0%

commit v1 on v0

v1 whole, which is shorter than its diff:
```python
import functools

import jax
import jax.numpy as jnp
from jax import lax
from jax.experimental import pallas as pl
from jax.experimental.pallas import tpu as pltpu
from jax.sharding import Mesh
from jax.sharding import PartitionSpec as P

NWIN = 4
AXES = ("wide_0", "wide_1", "wide_2", "narrow_0", "narrow_1", "narrow_2")
NARROW = AXES[3:]
WIDE = AXES[:3]
PLANE = ("wide_0", "narrow_2", "wide_2", "narrow_1")
RING = ("wide_1", "narrow_0")
HI = lax.Precision.HIGHEST
F32 = jnp.float32
BF16 = jnp.bfloat16


def iota(shape, dim):
    return lax.broadcasted_iota(jnp.int32, shape, dim)


def total_of(parts):
    while len(parts) > 1:
        parts = [a + b for a, b in zip(parts[::2], parts[1::2])] + parts[len(parts) & ~1 :]
    return parts[0]


def sweep(curv, chores):
    full = (8, 128)
    lane, sub = iota(full, 1), iota(full, 0)
    rows = [curv[8 * k : 8 * k + 8, :] for k in range(16)]
    for k in range(16):
        panel = rows[k]
        cols = [jnp.broadcast_to(panel[:, 8 * k + j : 8 * k + j + 1], full) for j in range(8)]
        held = {}
        for j in range(8):
            for i in range(j + 1):
                held[i, j] = jnp.broadcast_to(cols[j][i : i + 1, :], full)

        def at(i, j):
            return held[min(i, j), max(i, j)]

        for t in range(0, 8, 2):
            a, b, d = at(t, t), at(t, t + 1), at(t + 1, t + 1)
            det = 1.0 / (a * d - b * b)
            rest = [i for i in range(8) if i not in (t, t + 1)]
            one = {i: at(i, t) for i in rest}
            two = {i: at(i, t + 1) for i in rest}
            new_one = {i: (d * one[i] - b * two[i]) * det for i in rest}
            new_two = {i: (a * two[i] - b * one[i]) * det for i in rest}
            for j in rest:
                for i in rest:
                    if i <= j:
                        held[i, j] = held[i, j] - (one[i] * new_one[j] + two[i] * new_two[j])
            for i in rest:
                held[min(i, t), max(i, t)] = new_one[i]
                held[min(i, t + 1), max(i, t + 1)] = new_two[i]
            held[t, t], held[t, t + 1], held[t + 1, t + 1] = -d * det, b * det, -a * det
        columns = []
        for u in range(8):
            layer = [at(i, u) for i in range(8)]
            for bit in (1, 2, 4):
                layer = [
                    jnp.where((sub & bit) == 0, low, high) for low, high in zip(layer[::2], layer[1::2])
                ]
            columns.append(layer[0])
        inside = (lane // 8) == k
        panel = jnp.where(inside, jnp.where(lane % 8 == sub, 1.0, 0.0), panel)
        panel = -total_of([columns[u] * panel[u : u + 1, :] for u in range(8)])
        spread = [jnp.broadcast_to(panel[u : u + 1, :], full) for u in range(8)]
        for o in list(range(k + 1, 16)) + list(range(k)):
            was = rows[o]
            parts = [
                jnp.broadcast_to(was[:, 8 * k + u : 8 * k + u + 1], full) * spread[u] for u in range(8)
            ]
            rows[o] = jnp.where(inside, 0.0, was) - total_of(parts)
        rows[k] = panel
        for chore in chores[k]:
            chore()
    return jnp.concatenate(rows, axis=0)


def pick_lanes(pieces):
    place = iota(pieces[0].shape, 1) // 32
    out = pieces[3]
    for b in (2, 1, 0):
        out = jnp.where(place == b, pieces[b], out)
    return out


def roll32(value, by):
    by %= 4
    return value if by == 0 else pltpu.roll(value, by * 32, 1)


def dot(left, right, precision=HI):
    return jnp.dot(left, right, precision=precision, preferred_element_type=F32)


def halves(value):
    high = value.astype(BF16)
    return high, (value - high.astype(F32)).astype(BF16)


def assemble_kernel(count, window, weight, resid, local, glob, out, *scratch):
    wv, rv, lv, gv, gp, up, gh, gl, matrix, sems = scratch
    copies = [
        pltpu.make_async_copy(source, target, sems.at[n])
        for n, (source, target) in enumerate(((local, lv), (weight, wv), (resid, rv), (glob, gv)))
    ]
    for copy in copies:
        copy.start()
    for copy in copies[:3]:
        copy.wait()
    live = jnp.where(iota((1, 512), 1) < count[0], wv[...], 0.0)
    vb = jnp.transpose(jnp.broadcast_to(live, (128, 512)))
    rb = jnp.transpose(jnp.broadcast_to(rv[...], (128, 512)))
    slopes = lv[...]
    wlt = jnp.transpose(slopes) * live
    curv = dot(wlt, slopes)
    curv = curv + jnp.where(iota((128, 128), 0) == iota((128, 128), 1), 1.0, 0.0)
    copies[3].wait()

    def permute(h):
        r = slice(h * 32, h * 32 + 32)
        for x in range(4):
            first = gv[r, x * 256 : x * 256 + 128]
            second = gv[r, x * 256 + 128 : x * 256 + 256]
            gp[r, x * 128 : x * 128 + 128] = pick_lanes(
                [first, roll32(first, -1), roll32(second, 2), roll32(second, 1)]
            )
            gp[r, 512 + x * 128 : 512 + x * 128 + 128] = pick_lanes(
                [roll32(first, -1), roll32(first, 2), roll32(second, 1), second]
            )

    def turn(k, c):
        cols, r = slice(c * 128, c * 128 + 128), slice(k * 128, k * 128 + 128)
        gh[cols, r], gl[cols, r] = halves(jnp.transpose(gp[r, cols]))

    def couple(c):
        cols = slice(c * 128, c * 128 + 128)
        up[:, cols] = dot(wlt, gp[:, cols])

    chores = [[] for _ in range(16)]
    for h in range(16):
        chores[h // 2].append(functools.partial(permute, h))
    for c in range(8):
        chores[8 + c].append(functools.partial(couple, c))
        for k in range(4):
            chores[8 + c].append(functools.partial(turn, k, c))
    inv = sweep(curv, chores)

    rhs = []
    for q in range(2):
        for jh in range(2):
            n = slice((q * 2 + jh) * 256, (q * 2 + jh) * 256 + 256)
            left = gp[:, n] - dot(slopes, dot(inv, up[:, n]))
            parts = [left[:, :128] * vb, left[:, 128:] * vb]
            rhs += [jnp.sum(part * rb, axis=0, keepdims=True) for part in parts]
            zh, zl = halves(jnp.concatenate(parts, axis=1))
            for p in range(2):
                for ih in range(2):
                    if (p == q and ih > jh) or (p != q and ih < jh):
                        continue
                    m = slice((p * 2 + ih) * 256, (p * 2 + ih) * 256 + 256)
                    matrix[m, n] = dot(gh[m, :], zh, None) + dot(gh[m, :], zl, None) + dot(gl[m, :], zh, None)

    place = iota((32, 128), 1) // 32
    below = iota((32, 128), 0) >= iota((32, 128), 1) % 32
    ondiag = iota((32, 128), 0) == iota((32, 128), 1) % 32
    sub8 = iota((8, 128), 0)
    own = jnp.broadcast_to(window[0].astype(F32), (8, 128))
    for x in range(4):
        for y in range(4):
            i = x * 4 + y
            pair = matrix[512 + i * 32 : 512 + i * 32 + 32, x * 128 : x * 128 + 128]
            held = jnp.where(ondiag & (place == y), pair, 0.0)
            edge = roll32(jnp.sum(held, axis=0, keepdims=True), -y)
            tails = []
            for b in range(2):
                sums = pick_lanes(
                    [
                        roll32(rhs[p * 4 + a * 2 + b], p * 2 + a - y)
                        for p in range(2)
                        for a in range(2)
                    ]
                )
                tails.append(jnp.where(sub8 == 0, sums, jnp.where(sub8 == 1, edge, own)))
            for q in range(2):
                dest = ((x * 4 + y) * 2 + q) * 2
                cols = slice(q * 512 + x * 128, q * 512 + x * 128 + 128)
                for z in range(4):
                    i = z * 4 + y
                    same = slice(q * 512 + i * 32, q * 512 + i * 32 + 32)
                    cross = slice((1 - q) * 512 + i * 32, (1 - q) * 512 + i * 32 + 32)
                    if i < x * 4:
                        tile = matrix[same, cols]
                    elif i > x * 4 + 3:
                        tile = matrix[cross, cols]
                    else:
                        j = place + x * 4
                        tile = jnp.where(
                            (j > i) | ((j == i) & below), matrix[same, cols], matrix[cross, cols]
                        )
                    out[dest + z % 2, z // 2 * 32 : z // 2 * 32 + 32, :] = tile
                for b in range(2):
                    out[dest + b, 64:72, :] = tails[b]


def windows_kernel(arrived, out):
    def sums(g):
        acc = [jnp.zeros((8, 128), F32) for _ in range(NWIN)]
        for s in range(64):
            block = arrived[s, pl.ds(g * 8, 8), :]
            which = jnp.broadcast_to(arrived[s, 66:67, :], (8, 128))
            for w in range(NWIN):
                acc[w] = acc[w] + jnp.where(which == float(w), block, 0.0)
        return acc

    def packed(acc, back):
        return pick_lanes([roll32(acc[w], w - back) for w in range(NWIN)])

    @pl.loop(0, 2)
    def _(a):
        for k in range(4):
            acc = sums(a * 4 + k)
            for h in range(4):
                out[h * 2 + a, k * 8 : k * 8 + 8, :] = packed(acc, h)

    acc = sums(8)
    sub = iota((8, 128), 0)
    edge = jnp.broadcast_to(packed(acc, 0)[1:2, :], (8, 128))
    for a in range(2):
        first = jnp.broadcast_to(packed(acc, a)[0:1, :], (8, 128))
        second = jnp.broadcast_to(packed(acc, 2 + a)[0:1, :], (8, 128))
        tail = jnp.where(sub == 0, first, jnp.where(sub == 1, second, edge))
        for h in range(4):
            out[h * 2 + a, 32:40, :] = tail


def ring_kernel(arrived, out):
    total = arrived[0]
    for s in range(1, 8):
        total = total + arrived[s]
    out[...] = total


def finish_kernel(mine, other, out, rhs):
    x, zh, q = lax.axis_index("wide_0"), lax.axis_index("wide_1"), lax.axis_index("wide_2")
    zl = lax.axis_index("narrow_0") * 2 + lax.axis_index("narrow_1")
    y = lax.axis_index("narrow_2")
    i, j = zl * 4 + y, x * 4 + zh
    diag = jnp.broadcast_to(i == j, (32, 32))
    half = jnp.where(i <= j, q, 1 - q)
    lower = jnp.broadcast_to(half == 0, (32, 32))
    a, b = iota((32, 32), 0), iota((32, 32), 1)
    turned = jnp.transpose(mine[0:32, :])
    for w in range(NWIN):
        cols = slice(w * 32, w * 32 + 32)
        held, theirs = mine[0:32, cols], other[0:32, cols]
        flip = turned[cols, :]
        edge = jnp.broadcast_to(mine[34:35, cols], (32, 32))
        own_part = jnp.where(diag & (a >= b), held, flip)
        other_part = jnp.where(diag & (a == b), edge, jnp.where(diag & (a > b), flip, theirs))
        out[w, :, 0:32] = jnp.where(lower, own_part, other_part)
        out[w, :, 32:64] = jnp.where(lower, other_part, own_part)
        rhs[w : w + 1, 0:32] = mine[32:33, cols]
        rhs[w : w + 1, 32:64] = mine[33:34, cols]


def vmem(count):
    return [pl.BlockSpec(memory_space=pltpu.VMEM)] * count


def turn_pairs():
    place = lambda x, zh, q, zl, y: (((x * 4 + zh) * 2 + q) * 4 + zl) * 4 + y
    pairs = []
    for x in range(4):
        for zh in range(4):
            for q in range(2):
                for zl in range(4):
                    for y in range(4):
                        i, j = zl * 4 + y, x * 4 + zh
                        p = q if i <= j else 1 - q
                        target = 1 - q if i == j else p
                        pairs.append((place(x, zh, q, zl, y), place(zl, y, target, x, zh)))
    return pairs


def on_device(local_slopes, global_slopes, residuals, weights, track_slot_count, windows):
    small = pltpu.CompilerParams(vmem_limit_bytes=8 << 20)
    big = pltpu.CompilerParams(vmem_limit_bytes=48 << 20)
    payload = pl.pallas_call(
        assemble_kernel,
        out_shape=jax.ShapeDtypeStruct((64, 72, 128), F32),
        in_specs=[pl.BlockSpec(memory_space=pltpu.SMEM)] * 2 + [pl.BlockSpec(memory_space=pltpu.HBM)] * 4,
        out_specs=vmem(1)[0],
        scratch_shapes=[
            pltpu.VMEM((1, 512), F32),
            pltpu.VMEM((1, 512), F32),
            pltpu.VMEM((512, 128), F32),
            pltpu.VMEM((512, 1024), F32),
            pltpu.VMEM((512, 1024), F32),
            pltpu.VMEM((128, 1024), F32),
            pltpu.VMEM((1024, 512), BF16),
            pltpu.VMEM((1024, 512), BF16),
            pltpu.VMEM((1024, 1024), F32),
            pltpu.SemaphoreType.DMA((4,)),
        ],
        compiler_params=big,
        name="assemble",
    )(
        track_slot_count,
        windows,
        *[
            pltpu.with_memory_space_constraint(value, pltpu.HBM)
            for value in (weights, residuals, local_slopes[0], global_slopes[0])
        ],
    )
    arrived = lax.all_to_all(payload, PLANE, split_axis=0, concat_axis=0, tiled=True)
    packed = pl.pallas_call(
        windows_kernel,
        out_shape=jax.ShapeDtypeStruct((8, 40, 128), F32),
        in_specs=vmem(1),
        out_specs=vmem(1)[0],
        compiler_params=big,
        name="window_sums",
    )(arrived)
    ring = lax.all_to_all(packed, RING, split_axis=0, concat_axis=0, tiled=True)
    mine = pl.pallas_call(
        ring_kernel,
        out_shape=jax.ShapeDtypeStruct((40, 128), F32),
        in_specs=vmem(1),
        out_specs=vmem(1)[0],
        compiler_params=small,
        name="ring_sums",
    )(ring)
    other = lax.ppermute(mine, AXES, turn_pairs())
    out, rhs = pl.pallas_call(
        finish_kernel,
        out_shape=(
            jax.ShapeDtypeStruct((NWIN, 32, 64), F32),
            jax.ShapeDtypeStruct((NWIN, 64), F32),
        ),
        in_specs=vmem(2),
        out_specs=tuple(vmem(2)),
        compiler_params=small,
        name="finish",
    )(mine, other)
    return jnp.transpose(out, (0, 2, 1)), rhs


def solution(mesh):
    split = Mesh(mesh.devices.reshape(4, 4, 2, 2, 2, 4), AXES)
    return jax.shard_map(
        on_device,
        mesh=split,
        in_specs=(
            P(AXES, None, None),
            P(AXES, None, None),
            P(AXES, None),
            P(AXES, None),
            P(AXES),
            P(AXES),
        ),
        out_specs=(
            P(None, NARROW, WIDE),
            P(None, NARROW),
        ),
        check_vma=False,
    )
```

time: 121 us -> 109 us (0.901)
  Pallas kernels: 25.6 us -> 19.1 us
  local copies, waits for them, and re-layouts: 4.5 us -> 0 us
  starting transfers between devices: 7.87 us -> 4.21 us
  waiting for transfers between devices: 9.11 us -> 12.6 us
    unnamed x10 -> x0, local copies, waits for them, and re-layouts: 4.5 us -> none
    pallas_call x2, Pallas kernels: 22.4 us -> 18.3 us  [the longest x1 17 us: on_device(): pl.pallas_call(assemble_kernel, out_shape=jax.ShapeDtypeStruct((64, 72, 1...]
    all_to_all x1, blocking collectives: 35.3 us -> 31.3 us  [on_device(): ring = lax.all_to_all(packed, RING, split_axis=0, concat_axis=0, tiled=True)]
    ppermute x1, starting transfers between devices: 7.87 us -> 4.21 us  [on_device(): other = lax.ppermute(mine, AXES, turn_pairs())]
    ppermute x1, waiting for transfers between devices: 9.11 us -> 12.6 us  [on_device(): other = lax.ppermute(mine, AXES, turn_pairs())]
    all_to_all x1, blocking collectives: 36.4 us -> 39.3 us  [on_device(): lax.all_to_all(payload, PLANE, split_axis=0, concat_axis=0, tiled=True)]
    pallas_call x1, Pallas kernels: 1.59 us -> 0.01 us  [on_device(): pl.pallas_call(ring_kernel, out_shape=jax.ShapeDtypeStruct((40, 128), F32...]
where the time goes in v1:
time: 109 us; the launch traced here: 108 us
  blocking collectives  70.6 us (65%)
  Pallas kernels  19.1 us (18%)
  waiting for transfers between devices  12.6 us (12%)
  starting transfers between devices  4.21 us (4%)
  between operations  1.94 us (2%)
    all_to_all x1, blocking collectives, on_device(): lax.all_to_all(payload, PLANE, split_axis=0, concat_axis=0, tiled=True)  39.3 us
    all_to_all x1, blocking collectives, on_device(): ring = lax.all_to_all(packed, RING, split_axis=0, concat_axis=0, tiled=True)  31.3 us
    pallas_call x1, Pallas kernels, on_device(): pl.pallas_call(assemble_kernel, out_shape=jax.ShapeDtypeStruct((64, 72, 1...  17 us
    ppermute x1, waiting for transfers between devices, on_device(): other = lax.ppermute(mine, AXES, turn_pairs())  12.6 us
    ppermute x1, starting transfers between devices, on_device(): other = lax.ppermute(mine, AXES, turn_pairs())  4.21 us
  transfers between devices with their start and end apart: 1, of which 1 were waited for; matrix products, arithmetic and copies ran while one was open for 0% of the time, Pallas kernels for 0%

profile of v1, /device:TPU:16, one launch (start us, length us, event | category | flops | bytes accessed | tf_op | source)
XLA Modules:
  0.0 108.5 jit_solution(3005605772965126271)
XLA Ops:
  1.9 17.0 %assemble.1 = f32[64,72,128]{2,1,0:T(8,128)S(1)} custom-call(s32[1]{0:T(128)S(6)} %copy.8.count, s32[1]{0:T(128)S(6)} %copy.9.window, f32[1,512]{1,0:T(1,128)} %weight.1, f32[1,512]{1,0:T(1,128)} %resid.1, f32[512,128]{1,0:T(8,128)} %bitcast.4, f32[512,1024]{1,0:T(8,128)} %bitcast.3), custom_call_target="tpu_custom_call" | custom-call | tf_op jit(solution)/shard_map/assemble/pallas_call | solution.py:297
  18.9 39.3 %all_to_all.10.arrived = f32[64,72,128]{2,1,0:T(8,128)S(1)} all-to-all(f32[64,72,128]{2,1,0:T(8,128)S(1)} %assemble.1), channel_id=1, replica_groups=mesh['wide_0'=4,'wide_1'=4,'wide_2'=2,'narrow_0'=2,'narrow_1'=2,'narrow_..., dimensions={0} | all-to-all | bytes 4718592 | tf_op jit(solution)/shard_map/all_to_all | solution.py:324
  58.2 1.3 %window_sums.1 = f32[8,40,128]{2,1,0:T(8,128)S(1)} custom-call(f32[64,72,128]{2,1,0:T(8,128)S(1)} %all_to_all.10.arrived), custom_call_target="tpu_custom_call" | custom-call | tf_op jit(solution)/shard_map/window_sums/pallas_call | solution.py:325
  59.5 31.3 %all_to_all.11.arrived = f32[8,40,128]{2,1,0:T(8,128)S(1)} all-to-all(f32[8,40,128]{2,1,0:T(8,128)S(1)} %window_sums.1), channel_id=1, replica_groups=mesh['wide_0'=4,'wide_1'=4,'wide_2'=2,'narrow_0'=2,'narrow_1'=2,'narrow_..., dimensions={0} | all-to-all | bytes 327680 | tf_op jit(solution)/shard_map/all_to_all | solution.py:333
  90.8 4.2 %collective-permute-start = (f32[40,128]{1,0:T(8,128)S(1)}, f32[40,128]{1,0:T(8,128)S(1)}, u32[]{:S(2)}, u32[]{:S(2)}) collective-permute-start(f32[40,128]{1,0:T(8,128)S(1)} %ring_sums.1.mine), channel_id=1, source_target_pairs={{0,16},{1,48},{2,80},{3,112},{4,144},{5,176},{6,208},{7,240},{8,27... | collective-permute-start | bytes 61448 | tf_op jit(solution)/shard_map/ppermute | solution.py:342
  95.0 12.6 %collective-permute-done.other = f32[40,128]{1,0:T(8,128)S(1)} collective-permute-done((f32[40,128]{1,0:T(8,128)S(1)}, f32[40,128]{1,0:T(8,128)S(1)}, u32[]{:S(2)}, u32[]{:S(2)}) %collective-permute-start) | collective-permute-done | bytes 20512 | tf_op jit(solution)/shard_map/ppermute | solution.py:342
  107.6 0.9 finish.1
  (1 shorter events, 0.0 us)
Async XLA Ops:
  90.8 16.8 %collective-permute-start = (f32[40,128]{1,0:T(8,128)S(1)}, f32[40,128]{1,0:T(8,128)S(1)}, u32[]{:S(2)}, u32[]{:S(2)}) collective-permute-start(f32[40,128]{1,0:T(8,128)S(1)} %ring_sums.1.mine), channel_id=1, source_target_pairs={{0,16},{1,48},{2,80},{3,112},{4,144},{5,176},{6,208},{7,240},{8,27... | collective-permute-start | bytes 61448 | tf_op jit(solution)/shard_map/ppermute | solution.py:342

commit v2 on v1

--- a/solution.py
+++ b/solution.py
@@ -29,10 +29,11 @@
     return parts[0]
 
 
-def sweep(curv, chores):
+def factor(curv, chores):
     full = (8, 128)
     lane, sub = iota(full, 1), iota(full, 0)
     rows = [curv[8 * k : 8 * k + 8, :] for k in range(16)]
+    lower, scaled = [], []
     for k in range(16):
         panel = rows[k]
         cols = [jnp.broadcast_to(panel[:, 8 * k + j : 8 * k + j + 1], full) for j in range(8)]
@@ -70,18 +71,19 @@
             columns.append(layer[0])
         inside = (lane // 8) == k
         panel = jnp.where(inside, jnp.where(lane % 8 == sub, 1.0, 0.0), panel)
+        lower.append(jnp.where(lane < 8 * k + 8, panel, 0.0))
         panel = -total_of([columns[u] * panel[u : u + 1, :] for u in range(8)])
         spread = [jnp.broadcast_to(panel[u : u + 1, :], full) for u in range(8)]
-        for o in list(range(k + 1, 16)) + list(range(k)):
+        for o in range(k + 1, 16):
             was = rows[o]
             parts = [
                 jnp.broadcast_to(was[:, 8 * k + u : 8 * k + u + 1], full) * spread[u] for u in range(8)
             ]
             rows[o] = jnp.where(inside, 0.0, was) - total_of(parts)
-        rows[k] = panel
+        scaled.append(jnp.where(lane < 8 * k + 8, panel, 0.0))
         for chore in chores[k]:
             chore()
-    return jnp.concatenate(rows, axis=0)
+    return jnp.concatenate(lower, axis=0), jnp.concatenate(scaled, axis=0)
 
 
 def pick_lanes(pieces):
@@ -107,7 +109,7 @@
 
 
 def assemble_kernel(count, window, weight, resid, local, glob, out, *scratch):
-    wv, rv, lv, gv, gp, up, gh, gl, matrix, sems = scratch
+    wv, rv, lv, gv, gp, right, turned, middle, stack, matrix, sems = scratch
     copies = [
         pltpu.make_async_copy(source, target, sems.at[n])
         for n, (source, target) in enumerate(((local, lv), (weight, wv), (resid, rv), (glob, gv)))
@@ -117,7 +119,6 @@
     for copy in copies[:3]:
         copy.wait()
     live = jnp.where(iota((1, 512), 1) < count[0], wv[...], 0.0)
-    vb = jnp.transpose(jnp.broadcast_to(live, (128, 512)))
     rb = jnp.transpose(jnp.broadcast_to(rv[...], (128, 512)))
     slopes = lv[...]
     wlt = jnp.transpose(slopes) * live
@@ -130,44 +131,63 @@
         for x in range(4):
             first = gv[r, x * 256 : x * 256 + 128]
             second = gv[r, x * 256 + 128 : x * 256 + 256]
-            gp[r, x * 128 : x * 128 + 128] = pick_lanes(
-                [first, roll32(first, -1), roll32(second, 2), roll32(second, 1)]
-            )
-            gp[r, 512 + x * 128 : 512 + x * 128 + 128] = pick_lanes(
-                [roll32(first, -1), roll32(first, 2), roll32(second, 1), second]
-            )
+            even = pick_lanes([first, roll32(first, -1), roll32(second, 2), roll32(second, 1)])
+            odd = pick_lanes([roll32(first, -1), roll32(first, 2), roll32(second, 1), second])
+            for value, start in ((even, x * 128), (odd, 512 + x * 128)):
+                cols = slice(start, start + 128)
+                gp[r, cols] = value
+                high, low = halves(value)
+                right[h * 32 : h * 32 + 32, cols] = high
+                right[512 + h * 32 : 512 + h * 32 + 32, cols] = low
+                right[1024 + h * 32 : 1024 + h * 32 + 32, cols] = high
 
     def turn(k, c):
-        cols, r = slice(c * 128, c * 128 + 128), slice(k * 128, k * 128 + 128)
-        gh[cols, r], gl[cols, r] = halves(jnp.transpose(gp[r, cols]))
-
-    def couple(c):
         cols = slice(c * 128, c * 128 + 128)
-        up[:, cols] = dot(wlt, gp[:, cols])
+        high, low = halves(jnp.transpose(gp[k * 128 : k * 128 + 128, cols]))
+        for place, value in enumerate((high, high, low)):
+            turned[cols, place * 512 + k * 128 : place * 512 + k * 128 + 128] = value
 
     chores = [[] for _ in range(16)]
     for h in range(16):
         chores[h // 2].append(functools.partial(permute, h))
     for c in range(8):
-        chores[8 + c].append(functools.partial(couple, c))
         for k in range(4):
             chores[8 + c].append(functools.partial(turn, k, c))
-    inv = sweep(curv, chores)
-
+    wl = jnp.transpose(wlt)
+    lower, scaled = factor(curv, chores)
+
+    solved = dot(scaled, wlt)
+    forward = lax.dot_general(
+        wl, lower, (((1,), (1,)), ((), ())), precision=HI, preferred_element_type=F32
+    )
+    for k in range(4):
+        r = slice(k * 128, k * 128 + 128)
+        same = iota((128, 512), 0) + k * 128 == iota((128, 512), 1)
+        high, low = halves(jnp.where(same, live, 0.0) - dot(forward[r], solved))
+        for place, value in enumerate((high, high, low)):
+            middle[r, place * 512 : place * 512 + 512] = value
+
+    for c in range(4):
+        cols = slice(c * 256, c * 256 + 256)
+        gv[:, cols] = dot(middle[...], right[:, cols], None)
     rhs = []
+    for c in range(8):
+        cols = slice(c * 128, c * 128 + 128)
+        left = gv[:, cols]
+        rhs.append(jnp.sum(left * rb, axis=0, keepdims=True))
+        high, low = halves(left)
+        for place, value in enumerate((high, low, high)):
+            stack[place * 512 : place * 512 + 512, cols] = value
+
     for q in range(2):
         for jh in range(2):
             n = slice((q * 2 + jh) * 256, (q * 2 + jh) * 256 + 256)
-            left = gp[:, n] - dot(slopes, dot(inv, up[:, n]))
-            parts = [left[:, :128] * vb, left[:, 128:] * vb]
-            rhs += [jnp.sum(part * rb, axis=0, keepdims=True) for part in parts]
-            zh, zl = halves(jnp.concatenate(parts, axis=1))
             for p in range(2):
                 for ih in range(2):
                     if (p == q and ih > jh) or (p != q and ih < jh):
                         continue
                     m = slice((p * 2 + ih) * 256, (p * 2 + ih) * 256 + 256)
-                    matrix[m, n] = dot(gh[m, :], zh, None) + dot(gh[m, :], zl, None) + dot(gl[m, :], zh, None)
+                    matrix[m, n] = dot(turned[m, :], stack[:, n], None)
 
     place = iota((32, 128), 1) // 32
     below = iota((32, 128), 0) >= iota((32, 128), 1) % 32
@@ -305,9 +325,10 @@
             pltpu.VMEM((512, 128), F32),
             pltpu.VMEM((512, 1024), F32),
             pltpu.VMEM((512, 1024), F32),
-            pltpu.VMEM((128, 1024), F32),
-            pltpu.VMEM((1024, 512), BF16),
-            pltpu.VMEM((1024, 512), BF16),
+            pltpu.VMEM((1536, 1024), BF16),
+            pltpu.VMEM((1024, 1536), BF16),
+            pltpu.VMEM((512, 1536), BF16),
+            pltpu.VMEM((1536, 1024), BF16),
             pltpu.VMEM((1024, 1024), F32),
             pltpu.SemaphoreType.DMA((4,)),
         ],

time: 109 us -> 105 us (0.963)
  Pallas kernels: 19.1 us -> 15.6 us
    pallas_call x1, Pallas kernels: 17 us -> 13.4 us  [on_device(): pl.pallas_call(assemble_kernel, out_shape=jax.ShapeDtypeStruct((64, 72, 1...]
where the time goes in v2:
time: 105 us
  blocking collectives  70.6 us (67%)
  Pallas kernels  15.6 us (15%)
  waiting for transfers between devices  12.6 us (12%)
  starting transfers between devices  4.21 us (4%)
  between operations  1.94 us (2%)
    all_to_all x1, blocking collectives, on_device(): lax.all_to_all(payload, PLANE, split_axis=0, concat_axis=0, tiled=True)  39.3 us
    all_to_all x1, blocking collectives, on_device(): ring = lax.all_to_all(packed, RING, split_axis=0, concat_axis=0, tiled=True)  31.3 us
    pallas_call x1, Pallas kernels, on_device(): pl.pallas_call(assemble_kernel, out_shape=jax.ShapeDtypeStruct((64, 72, 1...  13.4 us
    ppermute x1, waiting for transfers between devices, on_device(): other = lax.ppermute(mine, AXES, turn_pairs())  12.6 us
    ppermute x1, starting transfers between devices, on_device(): other = lax.ppermute(mine, AXES, turn_pairs())  4.21 us
  transfers between devices with their start and end apart: 1, of which 1 were waited for; matrix products, arithmetic and copies ran while one was open for 0% of the time, Pallas kernels for 0%

profile of v2, /device:TPU:16, one launch (start us, length us, event | category | flops | bytes accessed | tf_op | source)
XLA Modules:
  0.0 104.9 jit_solution(6007624770440132383)
XLA Ops:
  1.9 13.4 %assemble.1 = f32[64,72,128]{2,1,0:T(8,128)S(1)} custom-call(s32[1]{0:T(128)S(6)} %copy.8.count, s32[1]{0:T(128)S(6)} %copy.9.window, f32[1,512]{1,0:T(1,128)} %weight.1, f32[1,512]{1,0:T(1,128)} %resid.1, f32[512,128]{1,0:T(8,128)} %bitcast.4, f32[512,1024]{1,0:T(8,128)} %bitcast.3), custom_call_target="tpu_custom_call" | custom-call | tf_op jit(solution)/shard_map/assemble/pallas_call | solution.py:317
  15.4 39.3 %all_to_all.10.arrived = f32[64,72,128]{2,1,0:T(8,128)S(1)} all-to-all(f32[64,72,128]{2,1,0:T(8,128)S(1)} %assemble.1), channel_id=1, replica_groups=mesh['wide_0'=4,'wide_1'=4,'wide_2'=2,'narrow_0'=2,'narrow_1'=2,'narrow_..., dimensions={0} | all-to-all | bytes 4718592 | tf_op jit(solution)/shard_map/all_to_all | solution.py:345
  54.6 1.3 %window_sums.1 = f32[8,40,128]{2,1,0:T(8,128)S(1)} custom-call(f32[64,72,128]{2,1,0:T(8,128)S(1)} %all_to_all.10.arrived), custom_call_target="tpu_custom_call" | custom-call | tf_op jit(solution)/shard_map/window_sums/pallas_call | solution.py:346
  55.9 31.3 %all_to_all.11.arrived = f32[8,40,128]{2,1,0:T(8,128)S(1)} all-to-all(f32[8,40,128]{2,1,0:T(8,128)S(1)} %window_sums.1), channel_id=1, replica_groups=mesh['wide_0'=4,'wide_1'=4,'wide_2'=2,'narrow_0'=2,'narrow_1'=2,'narrow_..., dimensions={0} | all-to-all | bytes 327680 | tf_op jit(solution)/shard_map/all_to_all | solution.py:354
  87.3 4.2 %collective-permute-start = (f32[40,128]{1,0:T(8,128)S(1)}, f32[40,128]{1,0:T(8,128)S(1)}, u32[]{:S(2)}, u32[]{:S(2)}) collective-permute-start(f32[40,128]{1,0:T(8,128)S(1)} %ring_sums.1.mine), channel_id=1, source_target_pairs={{0,16},{1,48},{2,80},{3,112},{4,144},{5,176},{6,208},{7,240},{8,27... | collective-permute-start | bytes 61448 | tf_op jit(solution)/shard_map/ppermute | solution.py:363
  91.5 12.6 %collective-permute-done.other = f32[40,128]{1,0:T(8,128)S(1)} collective-permute-done((f32[40,128]{1,0:T(8,128)S(1)}, f32[40,128]{1,0:T(8,128)S(1)}, u32[]{:S(2)}, u32[]{:S(2)}) %collective-permute-start) | collective-permute-done | bytes 20512 | tf_op jit(solution)/shard_map/ppermute | solution.py:363
  104.1 0.9 finish.1
  (1 shorter events, 0.0 us)
Async XLA Ops:
  87.3 16.8 %collective-permute-start = (f32[40,128]{1,0:T(8,128)S(1)}, f32[40,128]{1,0:T(8,128)S(1)}, u32[]{:S(2)}, u32[]{:S(2)}) collective-permute-start(f32[40,128]{1,0:T(8,128)S(1)} %ring_sums.1.mine), channel_id=1, source_target_pairs={{0,16},{1,48},{2,80},{3,112},{4,144},{5,176},{6,208},{7,240},{8,27... | collective-permute-start | bytes 61448 | tf_op jit(solution)/shard_map/ppermute | solution.py:363

commit v3 on v2

--- a/solution.py
+++ b/solution.py
@@ -29,7 +29,7 @@
     return parts[0]
 
 
-def factor(curv, chores):
+def factor(curv, lines, chores):
     full = (8, 128)
     lane, sub = iota(full, 1), iota(full, 0)
     rows = [curv[8 * k : 8 * k + 8, :] for k in range(16)]
@@ -37,10 +37,12 @@
     for k in range(16):
         panel = rows[k]
         cols = [jnp.broadcast_to(panel[:, 8 * k + j : 8 * k + j + 1], full) for j in range(8)]
+        for j in range(8):
+            lines[k, j] = cols[j]
         held = {}
         for j in range(8):
             for i in range(j + 1):
-                held[i, j] = jnp.broadcast_to(cols[j][i : i + 1, :], full)
+                held[i, j] = jnp.broadcast_to(lines[k, j, i : i + 1, :], full)
 
         def at(i, j):
             return held[min(i, j), max(i, j)]
@@ -108,8 +110,15 @@
     return high, (value - high.astype(F32)).astype(BF16)
 
 
+def thirds(value):
+    high = value.astype(BF16)
+    rest = value - high.astype(F32)
+    mid = rest.astype(BF16)
+    return high, mid, (rest - mid.astype(F32)).astype(BF16)
+
+
 def assemble_kernel(count, window, weight, resid, local, glob, out, *scratch):
-    wv, rv, lv, gv, gp, right, turned, middle, stack, matrix, sems = scratch
+    wv, rv, lv, gv, gp, vg, turned, up, fore, back, stack, matrix, lines, sems = scratch
     copies = [
         pltpu.make_async_copy(source, target, sems.at[n])
         for n, (source, target) in enumerate(((local, lv), (weight, wv), (resid, rv), (glob, gv)))
@@ -119,6 +128,7 @@
     for copy in copies[:3]:
         copy.wait()
     live = jnp.where(iota((1, 512), 1) < count[0], wv[...], 0.0)
+    vb = jnp.transpose(jnp.broadcast_to(live, (128, 512)))
     rb = jnp.transpose(jnp.broadcast_to(rv[...], (128, 512)))
     slopes = lv[...]
     wlt = jnp.transpose(slopes) * live
@@ -136,16 +146,17 @@
             for value, start in ((even, x * 128), (odd, 512 + x * 128)):
                 cols = slice(start, start + 128)
                 gp[r, cols] = value
-                high, low = halves(value)
-                right[h * 32 : h * 32 + 32, cols] = high
-                right[512 + h * 32 : 512 + h * 32 + 32, cols] = low
-                right[1024 + h * 32 : 1024 + h * 32 + 32, cols] = high
+                vg[r, cols] = value * vb[r]
 
     def turn(k, c):
         cols = slice(c * 128, c * 128 + 128)
         high, low = halves(jnp.transpose(gp[k * 128 : k * 128 + 128, cols]))
         for place, value in enumerate((high, high, low)):
             turned[cols, place * 512 + k * 128 : place * 512 + k * 128 + 128] = value
+
+    def couple(c):
+        cols = slice(c * 256, c * 256 + 256)
+        up[:, cols] = dot(wlt, gp[:, cols])
 
     chores = [[] for _ in range(16)]
     for h in range(16):
@@ -153,27 +164,30 @@
     for c in range(8):
         for k in range(4):
             chores[8 + c].append(functools.partial(turn, k, c))
+    for c in range(4):
+        chores[8 + 2 * c].append(functools.partial(couple, c))
     wl = jnp.transpose(wlt)
-    lower, scaled = factor(curv, chores)
-
-    solved = dot(scaled, wlt)
+    lower, scaled = factor(curv, lines, chores)
+
     forward = lax.dot_general(
         wl, lower, (((1,), (1,)), ((), ())), precision=HI, preferred_element_type=F32
     )
-    for k in range(4):
-        r = slice(k * 128, k * 128 + 128)
-        same = iota((128, 512), 0) + k * 128 == iota((128, 512), 1)
-        high, low = halves(jnp.where(same, live, 0.0) - dot(forward[r], solved))
-        for place, value in enumerate((high, high, low)):
-            middle[r, place * 512 : place * 512 + 512] = value
-
+    high, mid, low = thirds(forward)
+    for place, value in enumerate((high, high, mid, mid, high, low)):
+        fore[:, place * 128 : place * 128 + 128] = value
     for c in range(4):
         cols = slice(c * 256, c * 256 + 256)
-        gv[:, cols] = dot(middle[...], right[:, cols], None)
+        high, mid, low = thirds(dot(scaled, up[:, cols]))
+        for place, value in enumerate((high, mid, high, mid, low, high)):
+            back[place * 128 : place * 128 + 128, cols] = value
+
+    for c in range(4):
+        cols = slice(c * 256, c * 256 + 256)
+        gv[:, cols] = dot(fore[...], back[:, cols], None)
     rhs = []
     for c in range(8):
         cols = slice(c * 128, c * 128 + 128)
-        left = gv[:, cols]
+        left = vg[:, cols] - gv[:, cols]
         rhs.append(jnp.sum(left * rb, axis=0, keepdims=True))
         high, low = halves(left)
         for place, value in enumerate((high, low, high)):
@@ -325,11 +339,14 @@
             pltpu.VMEM((512, 128), F32),
             pltpu.VMEM((512, 1024), F32),
             pltpu.VMEM((512, 1024), F32),
-            pltpu.VMEM((1536, 1024), BF16),
+            pltpu.VMEM((512, 1024), F32),
             pltpu.VMEM((1024, 1536), BF16),
-            pltpu.VMEM((512, 1536), BF16),
+            pltpu.VMEM((128, 1024), F32),
+            pltpu.VMEM((512, 768), BF16),
+            pltpu.VMEM((768, 1024), BF16),
             pltpu.VMEM((1536, 1024), BF16),
             pltpu.VMEM((1024, 1024), F32),
+            pltpu.VMEM((16, 8, 8, 128), F32),
             pltpu.SemaphoreType.DMA((4,)),
         ],
         compiler_params=big,

time: 105 us -> 103 us (0.981)
  Pallas kernels: 15.6 us -> 13.3 us
    pallas_call x1, Pallas kernels: 13.4 us -> 11.1 us  [on_device(): pl.pallas_call(assemble_kernel, out_shape=jax.ShapeDtypeStruct((64, 72, 1...]
where the time goes in v3:
time: 103 us
  blocking collectives  70.6 us (69%)
  Pallas kernels  13.3 us (13%)
  waiting for transfers between devices  12.6 us (12%)
  starting transfers between devices  4.21 us (4%)
  between operations  1.94 us (2%)
    all_to_all x1, blocking collectives, on_device(): lax.all_to_all(payload, PLANE, split_axis=0, concat_axis=0, tiled=True)  39.3 us
    all_to_all x1, blocking collectives, on_device(): ring = lax.all_to_all(packed, RING, split_axis=0, concat_axis=0, tiled=True)  31.3 us
    ppermute x1, waiting for transfers between devices, on_device(): other = lax.ppermute(mine, AXES, turn_pairs())  12.6 us
    pallas_call x1, Pallas kernels, on_device(): pl.pallas_call(assemble_kernel, out_shape=jax.ShapeDtypeStruct((64, 72, 1...  11.1 us
    ppermute x1, starting transfers between devices, on_device(): other = lax.ppermute(mine, AXES, turn_pairs())  4.21 us
  transfers between devices with their start and end apart: 1, of which 1 were waited for; matrix products, arithmetic and copies ran while one was open for 0% of the time, Pallas kernels for 0%

profile of v3, /device:TPU:16, one launch (start us, length us, event | category | flops | bytes accessed | tf_op | source)
XLA Modules:
  0.0 102.6 jit_solution(6187615315453329830)
XLA Ops:
  1.9 11.1 %assemble.1 = f32[64,72,128]{2,1,0:T(8,128)S(1)} custom-call(s32[1]{0:T(128)S(6)} %copy.8.count, s32[1]{0:T(128)S(6)} %copy.9.window, f32[1,512]{1,0:T(1,128)} %weight.1, f32[1,512]{1,0:T(1,128)} %resid.1, f32[512,128]{1,0:T(8,128)} %bitcast.4, f32[512,1024]{1,0:T(8,128)} %bitcast.3), custom_call_target="tpu_custom_call" | custom-call | tf_op jit(solution)/shard_map/assemble/pallas_call | solution.py:331
  13.1 39.3 %all_to_all.10.arrived = f32[64,72,128]{2,1,0:T(8,128)S(1)} all-to-all(f32[64,72,128]{2,1,0:T(8,128)S(1)} %assemble.1), channel_id=1, replica_groups=mesh['wide_0'=4,'wide_1'=4,'wide_2'=2,'narrow_0'=2,'narrow_1'=2,'narrow_..., dimensions={0} | all-to-all | bytes 4718592 | tf_op jit(solution)/shard_map/all_to_all | solution.py:362
  52.3 1.3 %window_sums.1 = f32[8,40,128]{2,1,0:T(8,128)S(1)} custom-call(f32[64,72,128]{2,1,0:T(8,128)S(1)} %all_to_all.10.arrived), custom_call_target="tpu_custom_call" | custom-call | tf_op jit(solution)/shard_map/window_sums/pallas_call | solution.py:363
  53.6 31.3 %all_to_all.11.arrived = f32[8,40,128]{2,1,0:T(8,128)S(1)} all-to-all(f32[8,40,128]{2,1,0:T(8,128)S(1)} %window_sums.1), channel_id=1, replica_groups=mesh['wide_0'=4,'wide_1'=4,'wide_2'=2,'narrow_0'=2,'narrow_1'=2,'narrow_..., dimensions={0} | all-to-all | bytes 327680 | tf_op jit(solution)/shard_map/all_to_all | solution.py:371
  85.0 4.2 %collective-permute-start = (f32[40,128]{1,0:T(8,128)S(1)}, f32[40,128]{1,0:T(8,128)S(1)}, u32[]{:S(2)}, u32[]{:S(2)}) collective-permute-start(f32[40,128]{1,0:T(8,128)S(1)} %ring_sums.1.mine), channel_id=1, source_target_pairs={{0,16},{1,48},{2,80},{3,112},{4,144},{5,176},{6,208},{7,240},{8,27... | collective-permute-start | bytes 61448 | tf_op jit(solution)/shard_map/ppermute | solution.py:380
  89.2 12.6 %collective-permute-done.other = f32[40,128]{1,0:T(8,128)S(1)} collective-permute-done((f32[40,128]{1,0:T(8,128)S(1)}, f32[40,128]{1,0:T(8,128)S(1)}, u32[]{:S(2)}, u32[]{:S(2)}) %collective-permute-start) | collective-permute-done | bytes 20512 | tf_op jit(solution)/shard_map/ppermute | solution.py:380
  101.8 0.9 finish.1
  (1 shorter events, 0.0 us)
Async XLA Ops:
  85.0 16.8 %collective-permute-start = (f32[40,128]{1,0:T(8,128)S(1)}, f32[40,128]{1,0:T(8,128)S(1)}, u32[]{:S(2)}, u32[]{:S(2)}) collective-permute-start(f32[40,128]{1,0:T(8,128)S(1)} %ring_sums.1.mine), channel_id=1, source_target_pairs={{0,16},{1,48},{2,80},{3,112},{4,144},{5,176},{6,208},{7,240},{8,27... | collective-permute-start | bytes 61448 | tf_op jit(solution)/shard_map/ppermute | solution.py:380

commit v4 on v3

--- a/solution.py
+++ b/solution.py
@@ -181,52 +181,41 @@
         for place, value in enumerate((high, mid, high, mid, low, high)):
             back[place * 128 : place * 128 + 128, cols] = value
 
-    for c in range(4):
-        cols = slice(c * 256, c * 256 + 256)
+    rhs = []
+
+    def solved(n):
+        cols = slice(n * 256, n * 256 + 256)
         gv[:, cols] = dot(fore[...], back[:, cols], None)
-    rhs = []
-    for c in range(8):
-        cols = slice(c * 128, c * 128 + 128)
-        left = vg[:, cols] - gv[:, cols]
-        rhs.append(jnp.sum(left * rb, axis=0, keepdims=True))
-        high, low = halves(left)
-        for place, value in enumerate((high, low, high)):
-            stack[place * 512 : place * 512 + 512, cols] = value
-
-    for q in range(2):
-        for jh in range(2):
-            n = slice((q * 2 + jh) * 256, (q * 2 + jh) * 256 + 256)
-            for p in range(2):
-                for ih in range(2):
-                    if (p == q and ih > jh) or (p != q and ih < jh):
-                        continue
-                    m = slice((p * 2 + ih) * 256, (p * 2 + ih) * 256 + 256)
-                    matrix[m, n] = dot(turned[m, :], stack[:, n], None)
+
+    def subtract(n):
+        for c in (2 * n, 2 * n + 1):
+            cols = slice(c * 128, c * 128 + 128)
+            left = vg[:, cols] - gv[:, cols]
+            rhs.append(jnp.sum(left * rb, axis=0, keepdims=True))
+            high, low = halves(left)
+            for place, value in enumerate((high, low, high)):
+                stack[place * 512 : place * 512 + 512, cols] = value
+
+    def multiply(n):
+        q, jh = n // 2, n % 2
+        cols = slice(n * 256, n * 256 + 256)
+        for p in range(2):
+            for ih in range(2):
+                if (p == q and ih > jh) or (p != q and ih < jh):
+                    continue
+                m = slice((p * 2 + ih) * 256, (p * 2 + ih) * 256 + 256)
+                matrix[m, cols] = dot(turned[m, :], stack[:, cols], None)
 
     place = iota((32, 128), 1) // 32
     below = iota((32, 128), 0) >= iota((32, 128), 1) % 32
     ondiag = iota((32, 128), 0) == iota((32, 128), 1) % 32
-    sub8 = iota((8, 128), 0)
-    own = jnp.broadcast_to(window[0].astype(F32), (8, 128))
-    for x in range(4):
-        for y in range(4):
-            i = x * 4 + y
-            pair = matrix[512 + i * 32 : 512 + i * 32 + 32, x * 128 : x * 128 + 128]
-            held = jnp.where(ondiag & (place == y), pair, 0.0)
-            edge = roll32(jnp.sum(held, axis=0, keepdims=True), -y)
-            tails = []
-            for b in range(2):
-                sums = pick_lanes(
-                    [
-                        roll32(rhs[p * 4 + a * 2 + b], p * 2 + a - y)
-                        for p in range(2)
-                        for a in range(2)
-                    ]
-                )
-                tails.append(jnp.where(sub8 == 0, sums, jnp.where(sub8 == 1, edge, own)))
-            for q in range(2):
+
+    def pack(n):
+        q = n // 2
+        for x in (n % 2 * 2, n % 2 * 2 + 1):
+            cols = slice(q * 512 + x * 128, q * 512 + x * 128 + 128)
+            for y in range(4):
                 dest = ((x * 4 + y) * 2 + q) * 2
-                cols = slice(q * 512 + x * 128, q * 512 + x * 128 + 128)
                 for z in range(4):
                     i = z * 4 + y
                     same = slice(q * 512 + i * 32, q * 512 + i * 32 + 32)
@@ -241,18 +230,51 @@
                             (j > i) | ((j == i) & below), matrix[same, cols], matrix[cross, cols]
                         )
                     out[dest + z % 2, z // 2 * 32 : z // 2 * 32 + 32, :] = tile
-                for b in range(2):
-                    out[dest + b, 64:72, :] = tails[b]
+
+    solved(0)
+    solved(1)
+    subtract(0)
+    for n in range(4):
+        if n < 2:
+            solved(n + 2)
+        multiply(n)
+        if n < 3:
+            subtract(n + 1)
+        if n > 0:
+            pack(n - 1)
+    pack(3)
+
+    sub8 = iota((8, 128), 0)
+    own = jnp.broadcast_to(window[0].astype(F32), (8, 128))
+    for x in range(4):
+        for y in range(4):
+            i = x * 4 + y
+            pair = matrix[512 + i * 32 : 512 + i * 32 + 32, x * 128 : x * 128 + 128]
+            kept = jnp.where(ondiag & (place == y), pair, 0.0)
+            edge = roll32(jnp.sum(kept, axis=0, keepdims=True), -y)
+            for b in range(2):
+                sums = pick_lanes(
+                    [
+                        roll32(rhs[p * 4 + a * 2 + b], p * 2 + a - y)
+                        for p in range(2)
+                        for a in range(2)
+                    ]
+                )
+                tail = jnp.where(sub8 == 0, sums, jnp.where(sub8 == 1, edge, own))
+                for q in range(2):
+                    out[((x * 4 + y) * 2 + q) * 2 + b, 64:72, :] = tail
 
 
 def windows_kernel(arrived, out):
-    def sums(g):
-        acc = [jnp.zeros((8, 128), F32) for _ in range(NWIN)]
+    def sums(groups):
+        acc = [[jnp.zeros((8, 128), F32) for _ in range(NWIN)] for _ in groups]
         for s in range(64):
-            block = arrived[s, pl.ds(g * 8, 8), :]
             which = jnp.broadcast_to(arrived[s, 66:67, :], (8, 128))
-            for w in range(NWIN):
-                acc[w] = acc[w] + jnp.where(which == float(w), block, 0.0)
+            hits = [which == float(w) for w in range(NWIN)]
+            for n, g in enumerate(groups):
+                block = arrived[s, pl.ds(g * 8, 8), :]
+                for w in range(NWIN):
+                    acc[n][w] = acc[n][w] + jnp.where(hits[w], block, 0.0)
         return acc
 
     def packed(acc, back):
@@ -260,12 +282,11 @@
 
     @pl.loop(0, 2)
     def _(a):
-        for k in range(4):
-            acc = sums(a * 4 + k)
+        for k, acc in enumerate(sums([a * 4 + k for k in range(4)])):
             for h in range(4):
                 out[h * 2 + a, k * 8 : k * 8 + 8, :] = packed(acc, h)
 
-    acc = sums(8)
+    (acc,) = sums([8])
     sub = iota((8, 128), 0)
     edge = jnp.broadcast_to(packed(acc, 0)[1:2, :], (8, 128))
     for a in range(2):

time: 103 us -> 103 us (level)
  no operation moved by 1% of the time
where the time goes in v4:
time: 103 us; the launch traced here: 102 us
  blocking collectives  70.6 us (69%)
  Pallas kernels  13.1 us (13%)
  waiting for transfers between devices  12.6 us (12%)
  starting transfers between devices  4.21 us (4%)
  between operations  1.94 us (2%)
    all_to_all x1, blocking collectives, on_device(): lax.all_to_all(payload, PLANE, split_axis=0, concat_axis=0, tiled=True)  39.3 us
    all_to_all x1, blocking collectives, on_device(): ring = lax.all_to_all(packed, RING, split_axis=0, concat_axis=0, tiled=True)  31.3 us
    ppermute x1, waiting for transfers between devices, on_device(): other = lax.ppermute(mine, AXES, turn_pairs())  12.6 us
    pallas_call x1, Pallas kernels, on_device(): pl.pallas_call(assemble_kernel, out_shape=jax.ShapeDtypeStruct((64, 72, 1...  11 us
    ppermute x1, starting transfers between devices, on_device(): other = lax.ppermute(mine, AXES, turn_pairs())  4.21 us
  transfers between devices with their start and end apart: 1, of which 1 were waited for; matrix products, arithmetic and copies ran while one was open for 0% of the time, Pallas kernels for 0%

profile of v4, /device:TPU:16, one launch (start us, length us, event | category | flops | bytes accessed | tf_op | source)
XLA Modules:
  0.0 102.4 jit_solution(16147594660242658682)
XLA Ops:
  1.9 11.0 %assemble.1 = f32[64,72,128]{2,1,0:T(8,128)S(1)} custom-call(s32[1]{0:T(128)S(6)} %copy.8.count, s32[1]{0:T(128)S(6)} %copy.9.window, f32[1,512]{1,0:T(1,128)} %weight.1, f32[1,512]{1,0:T(1,128)} %resid.1, f32[512,128]{1,0:T(8,128)} %bitcast.4, f32[512,1024]{1,0:T(8,128)} %bitcast.3), custom_call_target="tpu_custom_call" | custom-call | tf_op jit(solution)/shard_map/assemble/pallas_call | solution.py:352
  12.9 39.3 %all_to_all.10.arrived = f32[64,72,128]{2,1,0:T(8,128)S(1)} all-to-all(f32[64,72,128]{2,1,0:T(8,128)S(1)} %assemble.1), channel_id=1, replica_groups=mesh['wide_0'=4,'wide_1'=4,'wide_2'=2,'narrow_0'=2,'narrow_1'=2,'narrow_..., dimensions={0} | all-to-all | bytes 4718592 | tf_op jit(solution)/shard_map/all_to_all | solution.py:383
  52.1 1.2 %window_sums.1 = f32[8,40,128]{2,1,0:T(8,128)S(1)} custom-call(f32[64,72,128]{2,1,0:T(8,128)S(1)} %all_to_all.10.arrived), custom_call_target="tpu_custom_call" | custom-call | tf_op jit(solution)/shard_map/window_sums/pallas_call | solution.py:384
  53.4 31.3 %all_to_all.11.arrived = f32[8,40,128]{2,1,0:T(8,128)S(1)} all-to-all(f32[8,40,128]{2,1,0:T(8,128)S(1)} %window_sums.1), channel_id=1, replica_groups=mesh['wide_0'=4,'wide_1'=4,'wide_2'=2,'narrow_0'=2,'narrow_1'=2,'narrow_..., dimensions={0} | all-to-all | bytes 327680 | tf_op jit(solution)/shard_map/all_to_all | solution.py:392
  84.8 4.2 %collective-permute-start = (f32[40,128]{1,0:T(8,128)S(1)}, f32[40,128]{1,0:T(8,128)S(1)}, u32[]{:S(2)}, u32[]{:S(2)}) collective-permute-start(f32[40,128]{1,0:T(8,128)S(1)} %ring_sums.1.mine), channel_id=1, source_target_pairs={{0,16},{1,48},{2,80},{3,112},{4,144},{5,176},{6,208},{7,240},{8,27... | collective-permute-start | bytes 61448 | tf_op jit(solution)/shard_map/ppermute | solution.py:401
  89.0 12.6 %collective-permute-done.other = f32[40,128]{1,0:T(8,128)S(1)} collective-permute-done((f32[40,128]{1,0:T(8,128)S(1)}, f32[40,128]{1,0:T(8,128)S(1)}, u32[]{:S(2)}, u32[]{:S(2)}) %collective-permute-start) | collective-permute-done | bytes 20512 | tf_op jit(solution)/shard_map/ppermute | solution.py:401
  101.5 0.9 finish.1
  (1 shorter events, 0.0 us)
Async XLA Ops:
  84.8 16.8 %collective-permute-start = (f32[40,128]{1,0:T(8,128)S(1)}, f32[40,128]{1,0:T(8,128)S(1)}, u32[]{:S(2)}, u32[]{:S(2)}) collective-permute-start(f32[40,128]{1,0:T(8,128)S(1)} %ring_sums.1.mine), channel_id=1, source_target_pairs={{0,16},{1,48},{2,80},{3,112},{4,144},{5,176},{6,208},{7,240},{8,27... | collective-permute-start | bytes 61448 | tf_op jit(solution)/shard_map/ppermute | solution.py:401
